TPU v7x, 32 devices: a whole 2x2x4 slice. The times are simulated.
32 devices in a mesh: items: 4 (over x, core), rows: 8 (over z, y).
Axes of the slice: x: 2, y: 2, z: 4, core: 2. Of those that a mesh axis runs over, the one named last changes fastest.
Arguments:
- tokens: bfloat16 [16384, 768], P(('items', 'rows')), may hold values from -6 to 6
- query_proj: bfloat16 [768, 768], P(('items', 'rows')), may hold values from -0.21875 to 0.21875
- key_proj: bfloat16 [768, 768], P(('items', 'rows')), may hold values from -0.21875 to 0.21875
- value_proj: bfloat16 [768, 768], P(('items', 'rows')), may hold values from -0.21875 to 0.21875
- query_bias: bfloat16 [768], P(('items', 'rows')), may hold values from -1.5 to 1.5
- value_bias: bfloat16 [768], P(('items', 'rows')), may hold values from -0.25 to 0.25
- output_proj: bfloat16 [768, 768], P(('items', 'rows')), may hold values from -0.875 to 0.875
- output_bias: bfloat16 [768], P(('items', 'rows')), may hold values from -1 to 1
- attn_gain: bfloat16 [768], P(('items', 'rows')), may hold values from 0.099609375 to 1.8984375
- attn_shift: bfloat16 [768], P(('items', 'rows')), may hold values from -1 to 1
- hidden_proj: bfloat16 [768, 3072], P(('items', 'rows')), may hold values from -0.21875 to 0.21875
- hidden_bias: bfloat16 [3072], P(('items', 'rows')), may hold values from -1 to 1
- return_proj: bfloat16 [3072, 768], P(('items', 'rows')), may hold values from -0.109375 to 0.109375
- return_bias: bfloat16 [768], P(('items', 'rows')), may hold values from -1 to 1
- final_gain: bfloat16 [768], P(('items', 'rows')), may hold values from 0.099609375 to 1.8984375
- final_shift: bfloat16 [768], P(('items', 'rows')), may hold values from -2.5 to 2.5
- item_lengths: int32 [4, 8], P('items'), may hold values from 1 to 1024, 4096 in all within a row
- out_grad: bfloat16 [16384, 768], P(('items', 'rows')), may hold values from -6 to 6
Outputs:
- layer_out: bfloat16 [16384, 768], P(('items', 'rows'))
- tokens_grad: float32 [16384, 768], P(('items', 'rows'))
- grad_query_proj: float32 [768, 768], P(('items', 'rows'))
- grad_key_proj: float32 [768, 768], P(('items', 'rows'))
- grad_value_proj: float32 [768, 768], P(('items', 'rows'))
- grad_query_bias: float32 [768], P(('items', 'rows'))
- grad_value_bias: float32 [768], P(('items', 'rows'))
- grad_output_proj: float32 [768, 768], P(('items', 'rows'))
- grad_output_bias: float32 [768], P(('items', 'rows'))
- grad_attn_gain: float32 [768], P(('items', 'rows'))
- grad_attn_shift: float32 [768], P(('items', 'rows'))
- grad_hidden_proj: float32 [768, 3072], P(('items', 'rows'))
- grad_hidden_bias: float32 [3072], P(('items', 'rows'))
- grad_return_proj: float32 [3072, 768], P(('items', 'rows'))
- grad_return_bias: float32 [768], P(('items', 'rows'))
- grad_final_gain: float32 [768], P(('items', 'rows'))
- grad_final_shift: float32 [768], P(('items', 'rows'))
Inputs may be any that keep to these rules, and one draw needn't show every extreme that they name: `item_lengths`: each row lists the lengths of its group's 8 items in stream order and sums to 4096; in each row one item has exactly 1024 tokens.
All inputs are finite; a program needn't handle non-finite values.
Results may differ from a plain program's by a relative error of at most 0.014.
Values may be sent and summed in bfloat16 or wider, within the bound.
A program may use at most 192 MiB of HBM per device.

v0:
```python
import jax
import jax.numpy as jnp
from jax import lax
from jax.sharding import PartitionSpec as P

H = 12
HEAD = 64
REACH = 2
WIN = 2560
eps_norm = 1e-06
masked_score = -1e30


def from_behind(value, axis, by):
    peers = lax.axis_size(axis)
    pairs = [(i, i + by) for i in range(peers) if 0 <= i + by < peers]
    return lax.ppermute(value, axis, pairs)


def dot_plain(matrix, factor):
    return jnp.dot(matrix, factor, preferred_element_type=jnp.float32)


def dot_rows(matrix, factor):
    return lax.dot_general(
        matrix, factor, (((0,), (0,)), ((), ())), preferred_element_type=jnp.float32
    )


def dot_cols(matrix, factor):
    return lax.dot_general(
        matrix, factor, (((1,), (1,)), ((), ())), preferred_element_type=jnp.float32
    )


def layer_norm(hidden, norm_gain, norm_shift):
    row_mean = jnp.mean(hidden, axis=1, keepdims=True)
    centred = hidden - row_mean
    row_var = jnp.mean(centred * centred, axis=1, keepdims=True)
    return centred * lax.rsqrt(row_var + eps_norm) * norm_gain + norm_shift


def gelu_exact(values):
    return jax.nn.gelu(values, approximate=False)


def segment_ids(row_lengths, first_row, num_rows):
    item_ends = jnp.cumsum(row_lengths, dtype=jnp.int32)
    places = first_row + jnp.arange(num_rows, dtype=jnp.int32)
    return jnp.sum(
        (places[:, None] >= item_ends[None, :]).astype(jnp.int32), axis=1, dtype=jnp.int32
    )


def split_heads(values):
    return values.reshape(values.shape[0], H, HEAD).transpose(1, 0, 2)


def join_heads(values):
    return values.transpose(1, 0, 2).reshape(values.shape[1], H * HEAD)


def widen_first(kv_pair):
    pieces = []
    for offset in range(-REACH, REACH + 1):
        if offset == 0:
            pieces.append(kv_pair)
        else:
            pieces.append(from_behind(kv_pair, "rows", -offset))
    return jnp.concatenate(pieces, axis=1)


def widen_again(kv_pair):
    pieces = []
    for offset in range(-REACH, REACH + 1):
        if offset == 0:
            pieces.append(kv_pair)
        else:
            pieces.append(from_behind(kv_pair, "rows", -offset))
    return jnp.concatenate(pieces, axis=1)


def collect(wide_grads):
    rows_dev = wide_grads.shape[1] // (2 * REACH + 1)
    summed = wide_grads[:, REACH * rows_dev : (REACH + 1) * rows_dev]
    for offset in range(-REACH, REACH + 1):
        if offset != 0:
            block_grads = wide_grads[
                :, (offset + REACH) * rows_dev : (offset + REACH + 1) * rows_dev
            ]
            summed = summed + from_behind(block_grads.astype(jnp.bfloat16), "rows", offset).astype(
                block_grads.dtype
            )
    return summed


def attend(query_rows, window, keep_mask):
    score_scale = HEAD ** (-0.5)

    def one_head(head_parts):
        head_query, head_keys, head_values = head_parts
        scores = jnp.where(keep_mask, dot_cols(head_query, head_keys) * score_scale, masked_score)
        row_max = jnp.max(scores, axis=1, keepdims=True)
        lifted = jnp.exp(scores - row_max)
        row_sum = jnp.sum(lifted, axis=1, keepdims=True)
        weights = (lifted / row_sum).astype(jnp.bfloat16)
        return (dot_plain(weights, head_values), (row_max + jnp.log(row_sum))[:, 0])

    outputs, logsum = lax.map(
        one_head, (split_heads(query_rows), split_heads(window[0]), split_heads(window[1]))
    )
    return (join_heads(outputs).astype(jnp.bfloat16), logsum)


def attend_back(query_rows, window, logsum, d_attended, keep_mask):
    score_scale = HEAD ** (-0.5)

    def one_head(head_parts):
        head_query, head_keys, head_values, head_logsum, head_grad = head_parts
        scores = jnp.where(keep_mask, dot_cols(head_query, head_keys) * score_scale, masked_score)
        weights = jnp.exp(scores - head_logsum[:, None])
        d_weights = dot_cols(head_grad, head_values)
        centre = jnp.sum(weights * d_weights, axis=1, keepdims=True)
        d_scores = (weights * (d_weights - centre)).astype(jnp.bfloat16)
        d_head_query = dot_plain(d_scores, head_keys) * score_scale
        d_head_keys = dot_rows(d_scores, head_query) * score_scale
        d_head_values = dot_rows(weights.astype(jnp.bfloat16), head_grad)
        return (d_head_query, d_head_keys, d_head_values)

    d_queries, d_keysets, d_valuesets = lax.map(
        one_head,
        (
            split_heads(query_rows),
            split_heads(window[0]),
            split_heads(window[1]),
            logsum,
            split_heads(d_attended),
        ),
    )
    return (
        join_heads(d_queries).astype(jnp.bfloat16),
        jnp.stack([join_heads(d_keysets), join_heads(d_valuesets)]),
    )


def forward(tokens, params, keep_mask, widen):
    (
        query_proj,
        key_proj,
        value_proj,
        query_bias,
        value_bias,
        output_proj,
        output_bias,
        attn_gain,
        attn_shift,
        hidden_proj,
        hidden_bias,
        return_proj,
        return_bias,
        final_gain,
        final_shift,
    ) = params
    query_rows = (dot_plain(tokens, query_proj) + query_bias.astype(jnp.float32)).astype(
        jnp.bfloat16
    )
    key_rows = dot_plain(tokens, key_proj).astype(jnp.bfloat16)
    value_rows = (dot_plain(tokens, value_proj) + value_bias.astype(jnp.float32)).astype(
        jnp.bfloat16
    )
    window = widen(jnp.stack([key_rows, value_rows]))
    attended, logsum = attend(query_rows, window, keep_mask)
    mixed = tokens.astype(jnp.float32) + (
        dot_plain(attended, output_proj) + output_bias.astype(jnp.float32)
    )
    normed = layer_norm(mixed, attn_gain.astype(jnp.float32), attn_shift.astype(jnp.float32))
    normed_low = normed.astype(jnp.bfloat16)
    hidden_pre = dot_plain(normed_low, hidden_proj) + hidden_bias.astype(jnp.float32)
    active = gelu_exact(hidden_pre).astype(jnp.bfloat16)
    second = normed + (dot_plain(active, return_proj) + return_bias.astype(jnp.float32))
    result = layer_norm(second, final_gain.astype(jnp.float32), final_shift.astype(jnp.float32))
    return (
        result,
        (
            query_rows,
            window,
            logsum,
            attended,
            mixed,
            normed,
            normed_low,
            hidden_pre,
            active,
            second,
        ),
    )


def backward(tokens, params, stored, out_grad, keep_mask):
    (
        query_proj,
        key_proj,
        value_proj,
        query_bias,
        value_bias,
        output_proj,
        output_bias,
        attn_gain,
        attn_shift,
        hidden_proj,
        hidden_bias,
        return_proj,
        return_bias,
        final_gain,
        final_shift,
    ) = params
    query_rows, window, logsum, attended, mixed, normed, normed_low, hidden_pre, active, second = (
        stored
    )
    ignored, final_back = jax.vjp(
        layer_norm, second, final_gain.astype(jnp.float32), final_shift.astype(jnp.float32)
    )
    d_second, grad_final_gain, grad_final_shift = final_back(out_grad.astype(jnp.float32))
    d_ffn = d_second.astype(jnp.bfloat16)
    grad_return_bias = jnp.sum(d_ffn.astype(jnp.float32), axis=0)
    grad_return_proj = dot_rows(active, d_ffn)
    ignored, gelu_back = jax.vjp(gelu_exact, hidden_pre)
    d_hidden = gelu_back(dot_cols(d_ffn, return_proj))[0].astype(jnp.bfloat16)
    grad_hidden_bias = jnp.sum(d_hidden.astype(jnp.float32), axis=0)
    grad_hidden_proj = dot_rows(normed_low, d_hidden)
    d_normed = dot_cols(d_hidden, hidden_proj) + d_second
    ignored, attn_back = jax.vjp(
        layer_norm, mixed, attn_gain.astype(jnp.float32), attn_shift.astype(jnp.float32)
    )
    d_mixed, grad_attn_gain, grad_attn_shift = attn_back(d_normed)
    d_branch = d_mixed.astype(jnp.bfloat16)
    grad_output_bias = jnp.sum(d_branch.astype(jnp.float32), axis=0)
    grad_output_proj = dot_rows(attended, d_branch)
    d_attended = dot_cols(d_branch, output_proj).astype(jnp.bfloat16)
    d_query, wide_grads = attend_back(query_rows, window, logsum, d_attended, keep_mask)
    key_value = collect(wide_grads)
    d_keys = key_value[0].astype(jnp.bfloat16)
    d_values = key_value[1].astype(jnp.bfloat16)
    grad_query_proj = dot_rows(tokens, d_query)
    grad_key_proj = dot_rows(tokens, d_keys)
    grad_value_proj = dot_rows(tokens, d_values)
    grad_query_bias = jnp.sum(d_query.astype(jnp.float32), axis=0)
    grad_value_bias = jnp.sum(d_values.astype(jnp.float32), axis=0)
    tokens_grad = (
        d_mixed
        + dot_cols(d_query, query_proj)
        + dot_cols(d_keys, key_proj)
        + dot_cols(d_values, value_proj)
    )
    return (
        tokens_grad,
        (
            grad_query_proj,
            grad_key_proj,
            grad_value_proj,
            grad_query_bias,
            grad_value_bias,
            grad_output_proj,
            grad_output_bias,
            grad_attn_gain,
            grad_attn_shift,
            grad_hidden_proj,
            grad_hidden_bias,
            grad_return_proj,
            grad_return_bias,
            grad_final_gain,
            grad_final_shift,
        ),
    )


def per_device(
    tokens,
    query_proj,
    key_proj,
    value_proj,
    query_bias,
    value_bias,
    output_proj,
    output_bias,
    attn_gain,
    attn_shift,
    hidden_proj,
    hidden_bias,
    return_proj,
    return_bias,
    final_gain,
    final_shift,
    item_lengths,
    out_grad,
):
    params = (
        lax.all_gather(query_proj, ("items", "rows"), axis=0, tiled=True),
        lax.all_gather(key_proj, ("items", "rows"), axis=0, tiled=True),
        lax.all_gather(value_proj, ("items", "rows"), axis=0, tiled=True),
        lax.all_gather(query_bias, ("items", "rows"), axis=0, tiled=True),
        lax.all_gather(value_bias, ("items", "rows"), axis=0, tiled=True),
        lax.all_gather(output_proj, ("items", "rows"), axis=0, tiled=True),
        lax.all_gather(output_bias, ("items", "rows"), axis=0, tiled=True),
        lax.all_gather(attn_gain, ("items", "rows"), axis=0, tiled=True),
        lax.all_gather(attn_shift, ("items", "rows"), axis=0, tiled=True),
        lax.all_gather(hidden_proj, ("items", "rows"), axis=0, tiled=True),
        lax.all_gather(hidden_bias, ("items", "rows"), axis=0, tiled=True),
        lax.all_gather(return_proj, ("items", "rows"), axis=0, tiled=True),
        lax.all_gather(return_bias, ("items", "rows"), axis=0, tiled=True),
        lax.all_gather(final_gain, ("items", "rows"), axis=0, tiled=True),
        lax.all_gather(final_shift, ("items", "rows"), axis=0, tiled=True),
    )
    rows_dev = tokens.shape[0]
    row_count = lax.axis_size("rows")
    position = lax.axis_index("rows") * rows_dev
    lengths_row = item_lengths[0]
    query_labels = segment_ids(lengths_row, position, rows_dev)
    window_first = position - REACH * rows_dev
    key_labels = segment_ids(lengths_row, window_first, WIN)
    key_places = window_first + jnp.arange(WIN, dtype=jnp.int32)
    inside = (key_places >= 0) & (key_places < row_count * rows_dev)
    keep_mask = (query_labels[:, None] == key_labels[None, :]) & inside[None, :]
    result, stored = forward(tokens, params, keep_mask, widen_first)
    fresh = lax.optimization_barrier((tokens, params, result))
    ignored, stored = forward(fresh[0], fresh[1], keep_mask, widen_again)
    tokens_grad, local_grads = backward(tokens, params, stored, out_grad, keep_mask)
    (
        grad_query_proj,
        grad_key_proj,
        grad_value_proj,
        grad_query_bias,
        grad_value_bias,
        grad_output_proj,
        grad_output_bias,
        grad_attn_gain,
        grad_attn_shift,
        grad_hidden_proj,
        grad_hidden_bias,
        grad_return_proj,
        grad_return_bias,
        grad_final_gain,
        grad_final_shift,
    ) = local_grads
    summed_grads = (
        lax.psum_scatter(grad_query_proj, ("items", "rows"), scatter_dimension=0, tiled=True),
        lax.psum_scatter(grad_key_proj, ("items", "rows"), scatter_dimension=0, tiled=True),
        lax.psum_scatter(grad_value_proj, ("items", "rows"), scatter_dimension=0, tiled=True),
        lax.psum_scatter(grad_query_bias, ("items", "rows"), scatter_dimension=0, tiled=True),
        lax.psum_scatter(grad_value_bias, ("items", "rows"), scatter_dimension=0, tiled=True),
        lax.psum_scatter(grad_output_proj, ("items", "rows"), scatter_dimension=0, tiled=True),
        lax.psum_scatter(grad_output_bias, ("items", "rows"), scatter_dimension=0, tiled=True),
        lax.psum_scatter(grad_attn_gain, ("items", "rows"), scatter_dimension=0, tiled=True),
        lax.psum_scatter(grad_attn_shift, ("items", "rows"), scatter_dimension=0, tiled=True),
        lax.psum_scatter(grad_hidden_proj, ("items", "rows"), scatter_dimension=0, tiled=True),
        lax.psum_scatter(grad_hidden_bias, ("items", "rows"), scatter_dimension=0, tiled=True),
        lax.psum_scatter(grad_return_proj, ("items", "rows"), scatter_dimension=0, tiled=True),
        lax.psum_scatter(grad_return_bias, ("items", "rows"), scatter_dimension=0, tiled=True),
        lax.psum_scatter(grad_final_gain, ("items", "rows"), scatter_dimension=0, tiled=True),
        lax.psum_scatter(grad_final_shift, ("items", "rows"), scatter_dimension=0, tiled=True),
    )
    return (
        result.astype(jnp.bfloat16),
        tokens_grad,
        summed_grads[0],
        summed_grads[1],
        summed_grads[2],
        summed_grads[3],
        summed_grads[4],
        summed_grads[5],
        summed_grads[6],
        summed_grads[7],
        summed_grads[8],
        summed_grads[9],
        summed_grads[10],
        summed_grads[11],
        summed_grads[12],
        summed_grads[13],
        summed_grads[14],
    )


def solution(mesh):
    return jax.shard_map(
        per_device,
        mesh=mesh,
        in_specs=(
            P(("items", "rows"), None),
            P(("items", "rows"), None),
            P(("items", "rows"), None),
            P(("items", "rows"), None),
            P(("items", "rows")),
            P(("items", "rows")),
            P(("items", "rows"), None),
            P(("items", "rows")),
            P(("items", "rows")),
            P(("items", "rows")),
            P(("items", "rows"), None),
            P(("items", "rows")),
            P(("items", "rows"), None),
            P(("items", "rows")),
            P(("items", "rows")),
            P(("items", "rows")),
            P("items", None),
            P(("items", "rows"), None),
        ),
        out_specs=(
            P(("items", "rows"), None),
            P(("items", "rows"), None),
            P(("items", "rows"), None),
            P(("items", "rows"), None),
            P(("items", "rows"), None),
            P(("items", "rows")),
            P(("items", "rows")),
            P(("items", "rows"), None),
            P(("items", "rows")),
            P(("items", "rows")),
            P(("items", "rows")),
            P(("items", "rows"), None),
            P(("items", "rows")),
            P(("items", "rows"), None),
            P(("items", "rows")),
            P(("items", "rows")),
            P(("items", "rows")),
        ),
        check_vma=False,
    )
```

profile of v0, /device:TPU:0, one launch (start us, length us, event | category | flops | bytes accessed | tf_op | source)
XLA Modules:
  0.0 1466.5 jit_solution(15196208716803237145)
XLA Ops:
  18.2 42.3 %all-reduce.19 = (bf16[3072]{0:T(1024)(128)(2,1)S(1)}, bf16[768]{0:T(1024)(128)(2,1)S(1)}, bf16[768]{0:T(1024)(128)(2,1)S(1)}, bf16[768]{0:T(1024)(128)(2,1)S(1)...) all-reduce(bf16[3072]{0:T(1024)(128)(2,1)S(1)} %dynamic-update-slic, ...), channel_id=1, replica_groups=mesh['items'=4,'rows'=8] {'items','rows'}, use_global_device_ids=true, to_apply=%add.5 | all-reduce | flops 9216 | bytes 36864
  70.2 53.8 %all-gather.11.cloned.1.call-done = bf16[768,768]{1,0:T(8,128)(2,1)} async-done(((bf16[24,768]{1,0:T(8,128)(2,1)}), bf16[768,768]{1,0:T(8,128)(2,1)}) %all-gather.11.cloned.1.call-update) | async-done | bytes 1179664 | tf_op jit(solution)/shard_map/all_gather | solution.py:300
  138.7 74.1 %all-gather.7.cloned.1.call-done = bf16[768,768]{1,0:T(8,128)(2,1)} async-done(((bf16[24,768]{1,0:T(8,128)(2,1)}), bf16[768,768]{1,0:T(8,128)(2,1)}) %all-gather.7.cloned.1.call-update) | async-done | bytes 1179664 | tf_op jit(solution)/shard_map/all_gather | solution.py:298
  239.3 66.2 %while.39 = (s32[]{:T(128)}, bf16[12,512,64]{1,2,0:T(8,128)(2,1)S(1)}, bf16[12,512,64]{1,2,0:T(8,128)(2,1)S(1)}, bf16[12,2560,64]{1,2,0:T(8,128)(2,1)}, bf16[12,...) while((s32[]{:T(128)}, ...), condition=%wide.region_6.7_spmd.clone, body=%wide.region_3.6_spmd.clone.sunk | while | flops 348650496 | bytes 16610397 | solution.py:109
  309.3 25.0 %all-gather.15.cloned.1.call-done = bf16[768,3072]{1,0:T(8,128)(2,1)} async-done(((bf16[24,3072]{1,0:T(8,128)(2,1)}), bf16[768,3072]{1,0:T(8,128)(2,1)}) %all-gather.15.cloned.1.call-update) | async-done | bytes 4718608 | tf_op jit(solution)/shard_map/all_gather | solution.py:307
  334.3 64.6 %all-gather.17.cloned.1.call-done = bf16[3072,768]{1,0:T(8,128)(2,1)} async-done(((bf16[96,768]{1,0:T(8,128)(2,1)}), bf16[3072,768]{1,0:T(8,128)(2,1)}) %all-gather.17.cloned.1.call-update) | async-done | bytes 4718608 | tf_op jit(solution)/shard_map/all_gather | solution.py:309
  398.9 22.1 %fusion.146 = (f32[512]{0:T(512)S(1)}, f32[512,768]{1,0:T(8,128)S(1)}) fusion(f32[768]{0:T(1024)S(1)} %convert_element_type.209, bf16[3072,768]{1,0:T(8,128)(2,1)} %all-gather.17.cloned.1.call-done, bf16[768,3072]{1,0:T(8,128)(2,1)} %all-gather.15.cloned.1.call-done, f32[3072]{0:T(1024)S(1)} %convert_element_type.207, f32[512,768]{1,0:T(8,128)} %copy-done.14, ...), kind=kOutput, calls=%fused_computation.239 | convolution fusion | flops 4940365312 | bytes 12610560 | tf_op jit(solution)/shard_map/dot_general | solution.py:21
  439.6 23.8 %collective-permute-done.4 = bf16[2,512,768]{2,1,0:T(8,128)(2,1)} collective-permute-done((bf16[2,512,768]{2,1,0:T(8,128)(2,1)}, bf16[2,512,768]{2,1,0:T(8,128)(2,1)}, u32[]{:S(2)}, u32[]{:S(2)}) %collective-permute-start.4) | collective-permute-done | bytes 1572896 | tf_op jit(solution)/shard_map/ppermute | solution.py:17
  464.9 36.5 %collective-permute-done.5 = bf16[2,512,768]{2,1,0:T(8,128)(2,1)} collective-permute-done((bf16[2,512,768]{2,1,0:T(8,128)(2,1)}, bf16[2,512,768]{2,1,0:T(8,128)(2,1)}, u32[]{:S(2)}, u32[]{:S(2)}) %collective-permute-start.5) | collective-permute-done | bytes 1572896 | tf_op jit(solution)/shard_map/ppermute | solution.py:17
  516.2 8.2 copy.95
  530.7 8.3 copy.96
  539.0 115.3 %while.40 = (s32[]{:T(128)}, bf16[12,512,64]{1,2,0:T(8,128)(2,1)S(1)}, f32[12,512]{1,0:T(8,128)S(1)}, bf16[12,512,64]{2,1,0:T(8,128)(2,1)S(1)}, bf16[12,2560,64]...) while((s32[]{:T(128)}, ...), condition=%wide.region_14.15_spmd.clone, body=%wide.region_11.14_spmd.clone.sunk | while | flops 348651008 | bytes 38313100 | solution.py:109
  657.8 20.1 %multiply_convert_fusion.1 = (bf16[512,3072]{1,0:T(8,128)(2,1)S(1)}, f32[512,3072]{1,0:T(8,128)}, f32[512,3072]{1,0:T(8,128)}) fusion(f32[3072]{0:T(1024)S(1)} %convert_element_type.226, bf16[768,3072]{1,0:T(8,128)(2,1)} %all-gather.15.cloned.1.call-done, f32[512,768]{1,0:T(8,128)S(1)} %get-tuple-element.516, f32[768]{0:T(1024)S(1)} %convert_element_type.224, ...), kind=kOutput, calls=%fused_computation.79 | convolution fusion | flops 2521694208 | bytes 22042624 | tf_op jit(solution)/shard_map/dot_general | solution.py:21
  682.8 8.3 convert_reduce_fusion
  703.1 151.0 %while.41 = (s32[]{:T(128)}, bf16[12,512,64]{1,2,0:T(8,128)(2,1)S(1)}, f32[12,2560,64]{1,2,0:T(8,128)}, f32[12,2560,64]{1,2,0:T(8,128)}, bf16[12,512,64]{2,1,0:T...) while((s32[]{:T(128)}, ...), condition=%wide.region_25.26_spmd.clone, body=%wide.region_23.25_spmd.clone.sunk | while | flops 853474816 | bytes 43153024 | solution.py:130
  859.5 9.8 fusion.56
  880.8 32.7 %collective-permute-done.10 = bf16[2,512,768]{1,2,0:T(8,128)(2,1)S(1)} collective-permute-done((bf16[2,512,768]{1,2,0:T(8,128)(2,1)S(1)}, bf16[2,512,768]{1,2,0:T(8,128)(2,1)S(1)}, u32[]{:S(2)}, u32[]{:S(2)}) %collective-permute-start.10) | collective-permute-done | bytes 1572896 | tf_op jit(solution)/shard_map/ppermute | solution.py:17
  936.2 8.4 fusion.153
  944.6 8.9 fusion.133
  958.6 76.0 %all-reduce.18 = (f32[768]{0:T(1024)S(1)}, f32[768]{0:T(1024)S(1)}, f32[768]{0:T(1024)S(1)}, f32[768]{0:T(1024)S(1)}, f32[768]{0:T(1024)S(1)}, /*index=5*/f32[30...) all-reduce(f32[768]{0:T(1024)S(1)} %reduce_sum.291, ...), channel_id=5, replica_groups=mesh['items'=4,'rows'=8] {'items','rows'}, use_global_device_ids=true, to_apply=%region_30.31.clone | all-reduce | flops 9216 | bytes 73728
  1044.3 27.5 %reduce-scatter.21.cloned.1.call-done = f32[24,768]{1,0:T(8,128)} async-done(((f32[768,768]{1,0:T(8,128)}), f32[24,768]{1,0:T(8,128)}) %reduce-scatter.21.cloned.1.call-update) | async-done | bytes 73744
  1071.8 104.4 %reduce-scatter.23.cloned.1.call-done = f32[24,768]{1,0:T(8,128)} async-done(((f32[768,768]{1,0:T(8,128)}), f32[24,768]{1,0:T(8,128)}) %reduce-scatter.23.cloned.1.call-update) | async-done | bytes 73744
  1176.1 141.8 %reduce-scatter.17.cloned.1.call-done = f32[96,768]{1,0:T(8,128)} async-done(((f32[3072,768]{1,0:T(8,128)}), f32[96,768]{1,0:T(8,128)}) %reduce-scatter.17.cloned.1.call-update) | async-done | bytes 294928 | tf_op jit(solution)/shard_map/reduce_scatter | solution.py:357
  1317.9 141.5 %reduce-scatter.15.cloned.1.call-done = f32[24,3072]{1,0:T(8,128)} async-done(((f32[768,3072]{1,0:T(8,128)}), f32[24,3072]{1,0:T(8,128)}) %reduce-scatter.15.cloned.1.call-update) | async-done | bytes 294928 | tf_op jit(solution)/shard_map/reduce_scatter | solution.py:355
  (432 shorter events, 511.3 us)
Async XLA Ops:
  7.2 60.7 %all-gather.9.cloned.1.call-start = ((), (), s32[]{:S(2)}) async-start(), calls=%async_computation.7 | async-start | bytes 1216512 | tf_op jit(solution)/shard_map/all_gather | solution.py:299
  7.9 116.1 %all-gather.11.cloned.1.call-start = ((), (), s32[]{:S(2)}) async-start(), calls=%async_computation.8 | async-start | bytes 1216512 | tf_op jit(solution)/shard_map/all_gather | solution.py:300
  8.7 204.1 %all-gather.7.cloned.1.call-start = ((), (), s32[]{:S(2)}) async-start(), calls=%async_computation.6 | async-start | bytes 1216512 | tf_op jit(solution)/shard_map/all_gather | solution.py:298
  9.4 296.2 %all-gather.13.cloned.1.call-start = ((), (), s32[]{:S(2)}) async-start(), calls=%async_computation.9 | async-start | bytes 1216512 | tf_op jit(solution)/shard_map/all_gather | solution.py:303
  10.0 324.3 %all-gather.15.cloned.1.call-start = ((), (), s32[]{:S(2)}) async-start(), calls=%async_computation.10 | async-start | bytes 4866048 | tf_op jit(solution)/shard_map/all_gather | solution.py:307
  10.6 388.3 %all-gather.17.cloned.1.call-start = ((), (), s32[]{:S(2)}) async-start(), calls=%async_computation.11 | async-start | bytes 4866048 | tf_op jit(solution)/shard_map/all_gather | solution.py:309
  127.4 89.8 %collective-permute-start = (bf16[2,512,768]{2,1,0:T(8,128)(2,1)}, bf16[2,512,768]{2,1,0:T(8,128)(2,1)}, u32[]{:S(2)}, u32[]{:S(2)}) collective-permute-start(bf16[2,512,768]{2,1,0:T(8,128)(2,1)} %pad_maximum_fusion.1), channel_id=1, source_target_pairs={{0,2},{1,3},{2,4},{3,5},{4,6},{5,7},{8,10},{9,11},{10,12},{11,13},... | collective-permute-start | bytes 4718600 | tf_op jit(solution)/shard_map/ppermute | solution.py:17
  131.0 87.7 %collective-permute-start.1 = (bf16[2,512,768]{2,1,0:T(8,128)(2,1)}, bf16[2,512,768]{2,1,0:T(8,128)(2,1)}, u32[]{:S(2)}, u32[]{:S(2)}) collective-permute-start(bf16[2,512,768]{2,1,0:T(8,128)(2,1)} %pad_maximum_fusion.1), channel_id=1, source_target_pairs={{0,1},{1,2},{2,3},{3,4},{4,5},{5,6},{6,7},{8,9},{9,10},{10,11},{11... | collective-permute-start | bytes 4718600 | tf_op jit(solution)/shard_map/ppermute | solution.py:17
  135.5 84.8 %collective-permute-start.2 = (bf16[2,512,768]{2,1,0:T(8,128)(2,1)}, bf16[2,512,768]{2,1,0:T(8,128)(2,1)}, u32[]{:S(2)}, u32[]{:S(2)}) collective-permute-start(bf16[2,512,768]{2,1,0:T(8,128)(2,1)} %pad_maximum_fusion.1), channel_id=1, source_target_pairs={{1,0},{2,1},{3,2},{4,3},{5,4},{6,5},{7,6},{9,8},{10,9},{11,10},{12... | collective-permute-start | bytes 4718600 | tf_op jit(solution)/shard_map/ppermute | solution.py:17
  136.8 85.0 %collective-permute-start.3 = (bf16[2,512,768]{2,1,0:T(8,128)(2,1)}, bf16[2,512,768]{2,1,0:T(8,128)(2,1)}, u32[]{:S(2)}, u32[]{:S(2)}) collective-permute-start(bf16[2,512,768]{2,1,0:T(8,128)(2,1)} %pad_maximum_fusion.1), channel_id=1, source_target_pairs={{2,0},{3,1},{4,2},{5,3},{6,4},{7,5},{10,8},{11,9},{12,10},{13,11},... | collective-permute-start | bytes 4718600 | tf_op jit(solution)/shard_map/ppermute | solution.py:17
  138.1 906.2 %reduce-scatter.13.cloned.1.call-start = ((), (), s32[]{:S(2)}) async-start(), calls=%async_computation.12 | async-start | bytes 2433024 | tf_op jit(solution)/shard_map/reduce_scatter | solution.py:351
  425.7 37.7 %collective-permute-start.4 = (bf16[2,512,768]{2,1,0:T(8,128)(2,1)}, bf16[2,512,768]{2,1,0:T(8,128)(2,1)}, u32[]{:S(2)}, u32[]{:S(2)}) collective-permute-start(bf16[2,512,768]{2,1,0:T(8,128)(2,1)} %pad_maximum_fusion.2), channel_id=1, source_target_pairs={{0,2},{1,3},{2,4},{3,5},{4,6},{5,7},{8,10},{9,11},{10,12},{11,13},... | collective-permute-start | bytes 4718600 | tf_op jit(solution)/shard_map/ppermute | solution.py:17
  430.1 71.2 %collective-permute-start.5 = (bf16[2,512,768]{2,1,0:T(8,128)(2,1)}, bf16[2,512,768]{2,1,0:T(8,128)(2,1)}, u32[]{:S(2)}, u32[]{:S(2)}) collective-permute-start(bf16[2,512,768]{2,1,0:T(8,128)(2,1)} %pad_maximum_fusion.2), channel_id=1, source_target_pairs={{0,1},{1,2},{2,3},{3,4},{4,5},{5,6},{6,7},{8,9},{9,10},{10,11},{11... | collective-permute-start | bytes 4718600 | tf_op jit(solution)/shard_map/ppermute | solution.py:17
  434.7 68.4 %collective-permute-start.6 = (bf16[2,512,768]{2,1,0:T(8,128)(2,1)}, bf16[2,512,768]{2,1,0:T(8,128)(2,1)}, u32[]{:S(2)}, u32[]{:S(2)}) collective-permute-start(bf16[2,512,768]{2,1,0:T(8,128)(2,1)} %pad_maximum_fusion.2), channel_id=1, source_target_pairs={{1,0},{2,1},{3,2},{4,3},{5,4},{6,5},{7,6},{9,8},{10,9},{11,10},{12... | collective-permute-start | bytes 4718600 | tf_op jit(solution)/shard_map/ppermute | solution.py:17
  436.0 69.2 %collective-permute-start.7 = (bf16[2,512,768]{2,1,0:T(8,128)(2,1)}, bf16[2,512,768]{2,1,0:T(8,128)(2,1)}, u32[]{:S(2)}, u32[]{:S(2)}) collective-permute-start(bf16[2,512,768]{2,1,0:T(8,128)(2,1)} %pad_maximum_fusion.2), channel_id=1, source_target_pairs={{2,0},{3,1},{4,2},{5,3},{6,4},{7,5},{10,8},{11,9},{12,10},{13,11},... | collective-permute-start | bytes 4718600 | tf_op jit(solution)/shard_map/ppermute | solution.py:17
  697.7 346.7 %reduce-scatter.19.cloned.1.call-start = ((), (), s32[]{:S(2)}) async-start(), calls=%async_computation.15 | async-start | bytes 2433024
  859.5 212.3 %reduce-scatter.21.cloned.1.call-start = ((), (), s32[]{:S(2)}) async-start(), calls=%async_computation.16 | async-start | bytes 2433024
  872.7 40.8 %collective-permute-start.10 = (bf16[2,512,768]{1,2,0:T(8,128)(2,1)S(1)}, bf16[2,512,768]{1,2,0:T(8,128)(2,1)S(1)}, u32[]{:S(2)}, u32[]{:S(2)}) collective-permute-start(bf16[2,512,768]{1,2,0:T(8,128)(2,1)S(1)} %get-tuple-element.505), channel_id=1, source_target_pairs={{0,1},{1,2},{2,3},{3,4},{4,5},{5,6},{6,7},{8,9},{9,10},{10,11},{11... | collective-permute-start | bytes 4718600 | tf_op jit(solution)/shard_map/ppermute | solution.py:17
  876.6 37.2 %collective-permute-start.11 = (bf16[2,512,768]{1,2,0:T(8,128)(2,1)S(1)}, bf16[2,512,768]{1,2,0:T(8,128)(2,1)S(1)}, u32[]{:S(2)}, u32[]{:S(2)}) collective-permute-start(bf16[2,512,768]{1,2,0:T(8,128)(2,1)S(1)} %get-tuple-element.504), channel_id=1, source_target_pairs={{0,2},{1,3},{2,4},{3,5},{4,6},{5,7},{8,10},{9,11},{10,12},{11,13},... | collective-permute-start | bytes 4718600 | tf_op jit(solution)/shard_map/ppermute | solution.py:17
  878.1 42.8 %collective-permute-start.8 = (bf16[2,512,768]{1,2,0:T(8,128)(2,1)S(1)}, bf16[2,512,768]{1,2,0:T(8,128)(2,1)S(1)}, u32[]{:S(2)}, u32[]{:S(2)}) collective-permute-start(bf16[2,512,768]{1,2,0:T(8,128)(2,1)S(1)} %get-tuple-element.503), channel_id=1, source_target_pairs={{2,0},{3,1},{4,2},{5,3},{6,4},{7,5},{10,8},{11,9},{12,10},{13,11},... | collective-permute-start | bytes 4718600 | tf_op jit(solution)/shard_map/ppermute | solution.py:17
  879.4 41.5 %collective-permute-start.9 = (bf16[2,512,768]{1,2,0:T(8,128)(2,1)S(1)}, bf16[2,512,768]{1,2,0:T(8,128)(2,1)S(1)}, u32[]{:S(2)}, u32[]{:S(2)}) collective-permute-start(bf16[2,512,768]{1,2,0:T(8,128)(2,1)S(1)} %get-tuple-element.506), channel_id=1, source_target_pairs={{1,0},{2,1},{3,2},{4,3},{5,4},{6,5},{7,6},{9,8},{10,9},{11,10},{12... | collective-permute-start | bytes 4718600 | tf_op jit(solution)/shard_map/ppermute | solution.py:17
  929.4 246.7 %reduce-scatter.23.cloned.1.call-start = ((), (), s32[]{:S(2)}) async-start(), calls=%async_computation.17 | async-start | bytes 2433024
  935.9 382.0 %reduce-scatter.17.cloned.1.call-start = ((), (), s32[]{:S(2)}) async-start(), calls=%async_computation.14 | async-start | bytes 9732096 | tf_op jit(solution)/shard_map/reduce_scatter | solution.py:357
  944.6 514.8 %reduce-scatter.15.cloned.1.call-start = ((), (), s32[]{:S(2)}) async-start(), calls=%async_computation.13 | async-start | bytes 9732096 | tf_op jit(solution)/shard_map/reduce_scatter | solution.py:355
  (38 other events, 589.4 us)
Sparse Core Ops, SparseCore 0:
  10.9 56.9 all-gather.8
  70.8 53.1 all-gather.10
  127.0 85.7 all-gather.6
  215.6 53.3 all-gather.12
  271.7 62.5 all-gather.14
  337.0 61.8 all-gather.16
  697.8 97.2 reduce-scatter.12
  859.6 107.6 reduce-scatter.18
  973.2 98.5 reduce-scatter.20
  1077.5 98.6 reduce-scatter.22
  1182.6 135.2 reduce-scatter.16
  1324.2 135.1 reduce-scatter.14
where the time goes:
time: 1480 us; the launch traced here: 1470 us
  waiting for transfers between devices  744 us (50%)
  matrix products  386 us (26%)
  local copies, waits for them, and re-layouts  121 us (8%)
  blocking collectives  118 us (8%)
  other arithmetic  49.4 us (3%)
  starting transfers between devices  31.1 us (2%)
  between operations  15.4 us (1%)
    dot_general x47, matrix products, dot_plain(): return jnp.dot(matrix, factor, preferred_element_type=jnp.float32)  155 us
    dot_general x54, matrix products, dot_cols(): lax.dot_general(matrix, factor, (((1,), (1,)), ((), ())), preferred_eleme...  148 us
    reduce_scatter x1, waiting for transfers between devices, per_device(): lax.psum_scatter(grad_return_proj, ('items', 'rows'), scatter_dimension=0...  142 us
    reduce_scatter x1, waiting for transfers between devices, per_device(): lax.psum_scatter(grad_hidden_proj, ('items', 'rows'), scatter_dimension=0...  142 us
    unnamed x15, waiting for transfers between devices  135 us
    unnamed x2, blocking collectives  118 us
    ppermute x12, waiting for transfers between devices, from_behind(): return lax.ppermute(value, axis, pairs)  101 us
    dot_general x30, matrix products, dot_rows(): lax.dot_general(matrix, factor, (((0,), (0,)), ((), ())), preferred_eleme...  82.9 us
  transfers between devices with their start and end apart: 24, of which 15 were waited for; matrix products, arithmetic and copies ran while one was open for 23% of the time, Pallas kernels for 0%

commit v1 on v0

--- a/solution.py
+++ b/solution.py
@@ -294,10 +294,20 @@
     item_lengths,
     out_grad,
 ):
+
+    def _deliver_run(x_local):
+        crops = []
+        for _ in range(lax.axis_size(("items", "rows"))):
+            crops.append(x_local)
+        small = jnp.stack(crops, 0)
+        long_array = lax.all_to_all(small, concat_axis=0, axis_name=("items", "rows"), split_axis=0)
+        res = jnp.concatenate(long_array, 0)
+        return res
+
     params = (
         lax.all_gather(query_proj, ("items", "rows"), axis=0, tiled=True),
         lax.all_gather(key_proj, ("items", "rows"), axis=0, tiled=True),
-        lax.all_gather(value_proj, ("items", "rows"), axis=0, tiled=True),
+        _deliver_run(value_proj),
         lax.all_gather(query_bias, ("items", "rows"), axis=0, tiled=True),
         lax.all_gather(value_bias, ("items", "rows"), axis=0, tiled=True),
         lax.all_gather(output_proj, ("items", "rows"), axis=0, tiled=True),

time: 1480 us -> 1430 us (0.966)
  waiting for transfers between devices: 744 us -> 681 us
    all_gather x1 -> x0, waiting for transfers between devices: 53.8 us -> none  [per_device(): lax.all_gather(value_proj, ('items', 'rows'), axis=0, tiled=True)]
    unnamed x91 -> x97, local copies, waits for them, and re-layouts: 50.3 us -> 51.2 us
    unnamed x15 -> x14, waiting for transfers between devices: 135 us -> 135 us
  transfers between devices with their start and end apart: 24 -> 24, of which waited for: 15 -> 14; matrix products, arithmetic and copies ran while one was open for 23% -> 24% of each run, Pallas kernels for 0% -> 0%
where the time goes in v1:
time: 1430 us; the launch traced here: 1410 us
  waiting for transfers between devices  681 us (48%)
  matrix products  385 us (27%)
  local copies, waits for them, and re-layouts  125 us (9%)
  blocking collectives  120 us (8%)
  other arithmetic  49.3 us (3%)
  starting transfers between devices  38.4 us (3%)
  between operations  15.1 us (1%)
    dot_general x47, matrix products, dot_plain(): return jnp.dot(matrix, factor, preferred_element_type=jnp.float32)  154 us
    dot_general x54, matrix products, dot_cols(): lax.dot_general(matrix, factor, (((1,), (1,)), ((), ())), preferred_eleme...  148 us
    reduce_scatter x1, waiting for transfers between devices, per_device(): lax.psum_scatter(grad_hidden_proj, ('items', 'rows'), scatter_dimension=0...  142 us
    reduce_scatter x1, waiting for transfers between devices, per_device(): lax.psum_scatter(grad_return_proj, ('items', 'rows'), scatter_dimension=0...  142 us
    unnamed x14, waiting for transfers between devices  135 us
    unnamed x2, blocking collectives  120 us
    ppermute x12, waiting for transfers between devices, from_behind(): return lax.ppermute(value, axis, pairs)  101 us
    dot_general x30, matrix products, dot_rows(): lax.dot_general(matrix, factor, (((0,), (0,)), ((), ())), preferred_eleme...  82.9 us
  transfers between devices with their start and end apart: 24, of which 14 were waited for; matrix products, arithmetic and copies ran while one was open for 24% of the time, Pallas kernels for 0%

profile of v1, /device:TPU:0, one launch (start us, length us, event | category | flops | bytes accessed | tf_op | source)
XLA Modules:
  0.0 1414.5 jit_solution(9441752144360628107)
XLA Ops:
  11.8 7.3 all-to-all-start
  26.8 43.6 %all-reduce.19 = (bf16[3072]{0:T(1024)(128)(2,1)S(1)}, bf16[768]{0:T(1024)(128)(2,1)S(1)}, bf16[768]{0:T(1024)(128)(2,1)S(1)}, bf16[768]{0:T(1024)(128)(2,1)S(1)...) all-reduce(bf16[3072]{0:T(1024)(128)(2,1)S(1)} %dynamic-update-slic, ...), channel_id=1, replica_groups=mesh['items'=4,'rows'=8] {'items','rows'}, use_global_device_ids=true, to_apply=%add.5 | all-reduce | flops 9216 | bytes 36864
  87.4 73.8 %all-gather.6.cloned.1.call-done = bf16[768,768]{1,0:T(8,128)(2,1)} async-done(((bf16[24,768]{1,0:T(8,128)(2,1)}), bf16[768,768]{1,0:T(8,128)(2,1)}) %all-gather.6.cloned.1.call-update) | async-done | bytes 1179664 | tf_op jit(solution)/shard_map/all_gather | solution.py:308
  188.8 66.8 %while.39 = (s32[]{:T(128)}, bf16[12,512,64]{1,2,0:T(8,128)(2,1)S(1)}, bf16[12,512,64]{1,2,0:T(8,128)(2,1)}, bf16[12,2560,64]{1,2,0:T(8,128)(2,1)}, bf16[12,2560...) while((s32[]{:T(128)}, ...), condition=%wide.region_6.7_spmd.clone, body=%wide.region_3.6_spmd.clone.sunk | while | flops 348650496 | bytes 16607837 | solution.py:109
  259.2 23.1 %all-gather.12.cloned.1.call-done = bf16[768,3072]{1,0:T(8,128)(2,1)} async-done(((bf16[24,3072]{1,0:T(8,128)(2,1)}), bf16[768,3072]{1,0:T(8,128)(2,1)}) %all-gather.12.cloned.1.call-update) | async-done | bytes 4718608 | tf_op jit(solution)/shard_map/all_gather | solution.py:317
  282.3 64.6 %all-gather.14.cloned.1.call-done = bf16[3072,768]{1,0:T(8,128)(2,1)} async-done(((bf16[96,768]{1,0:T(8,128)(2,1)}), bf16[3072,768]{1,0:T(8,128)(2,1)}) %all-gather.14.cloned.1.call-update) | async-done | bytes 4718608 | tf_op jit(solution)/shard_map/all_gather | solution.py:319
  346.9 22.1 %fusion.151 = (f32[512]{0:T(512)S(1)}, f32[512,768]{1,0:T(8,128)S(1)}) fusion(f32[768]{0:T(1024)S(1)} %convert_element_type.212, bf16[3072,768]{1,0:T(8,128)(2,1)} %all-gather.14.cloned.1.call-done, bf16[768,3072]{1,0:T(8,128)(2,1)} %all-gather.12.cloned.1.call-done, f32[3072]{0:T(1024)S(1)} %convert_element_type.210, f32[512,768]{1,0:T(8,128)} %copy-done.19, ...), kind=kOutput, calls=%fused_computation.240 | convolution fusion | flops 4940365312 | bytes 12610560 | tf_op jit(solution)/shard_map/dot_general | solution.py:21
  387.6 23.8 %collective-permute-done.4 = bf16[2,512,768]{2,1,0:T(8,128)(2,1)} collective-permute-done((bf16[2,512,768]{2,1,0:T(8,128)(2,1)}, bf16[2,512,768]{2,1,0:T(8,128)(2,1)}, u32[]{:S(2)}, u32[]{:S(2)}) %collective-permute-start.4) | collective-permute-done | bytes 1572896 | tf_op jit(solution)/shard_map/ppermute | solution.py:17
  412.9 36.5 %collective-permute-done.5 = bf16[2,512,768]{2,1,0:T(8,128)(2,1)} collective-permute-done((bf16[2,512,768]{2,1,0:T(8,128)(2,1)}, bf16[2,512,768]{2,1,0:T(8,128)(2,1)}, u32[]{:S(2)}, u32[]{:S(2)}) %collective-permute-start.5) | collective-permute-done | bytes 1572896 | tf_op jit(solution)/shard_map/ppermute | solution.py:17
  464.2 8.2 copy.95
  478.7 8.3 copy.96
  487.0 115.3 %while.40 = (s32[]{:T(128)}, bf16[12,512,64]{1,2,0:T(8,128)(2,1)S(1)}, f32[12,512]{1,0:T(8,128)S(1)}, bf16[12,512,64]{2,1,0:T(8,128)(2,1)S(1)}, bf16[12,2560,64]...) while((s32[]{:T(128)}, ...), condition=%wide.region_14.15_spmd.clone, body=%wide.region_11.14_spmd.clone.sunk | while | flops 348651008 | bytes 38313100 | solution.py:109
  605.8 20.1 %multiply_convert_fusion.1 = (bf16[512,3072]{1,0:T(8,128)(2,1)S(1)}, f32[512,3072]{1,0:T(8,128)}, f32[512,3072]{1,0:T(8,128)}) fusion(f32[3072]{0:T(1024)S(1)} %convert_element_type.229, bf16[768,3072]{1,0:T(8,128)(2,1)} %all-gather.12.cloned.1.call-done, f32[512,768]{1,0:T(8,128)S(1)} %get-tuple-element.516, f32[768]{0:T(1024)S(1)} %convert_element_type.227, ...), kind=kOutput, calls=%fused_computation.79 | convolution fusion | flops 2521694208 | bytes 22042624 | tf_op jit(solution)/shard_map/dot_general | solution.py:21
  630.8 8.3 convert_reduce_fusion
  651.1 151.2 %while.41 = (s32[]{:T(128)}, bf16[12,512,64]{1,2,0:T(8,128)(2,1)S(1)}, f32[12,2560,64]{1,2,0:T(8,128)}, f32[12,2560,64]{1,2,0:T(8,128)}, bf16[12,512,64]{2,1,0:T...) while((s32[]{:T(128)}, ...), condition=%wide.region_25.26_spmd.clone, body=%wide.region_23.25_spmd.clone.sunk | while | flops 853474816 | bytes 43153024 | solution.py:130
  807.7 9.8 fusion.56
  829.1 32.6 %collective-permute-done.10 = bf16[2,512,768]{1,2,0:T(8,128)(2,1)S(1)} collective-permute-done((bf16[2,512,768]{1,2,0:T(8,128)(2,1)S(1)}, bf16[2,512,768]{1,2,0:T(8,128)(2,1)S(1)}, u32[]{:S(2)}, u32[]{:S(2)}) %collective-permute-start.10) | collective-permute-done | bytes 1572896 | tf_op jit(solution)/shard_map/ppermute | solution.py:17
  884.4 8.4 fusion.158
  892.9 8.9 fusion.138
  906.9 75.9 %all-reduce.18 = (f32[768]{0:T(1024)S(1)}, f32[768]{0:T(1024)S(1)}, f32[768]{0:T(1024)S(1)}, f32[768]{0:T(1024)S(1)}, f32[768]{0:T(1024)S(1)}, /*index=5*/f32[30...) all-reduce(f32[768]{0:T(1024)S(1)} %reduce_sum.291, ...), channel_id=5, replica_groups=mesh['items'=4,'rows'=8] {'items','rows'}, use_global_device_ids=true, to_apply=%region_30.31.clone | all-reduce | flops 9216 | bytes 73728
  992.5 27.5 %reduce-scatter.21.cloned.1.call-done = f32[24,768]{1,0:T(8,128)} async-done(((f32[768,768]{1,0:T(8,128)}), f32[24,768]{1,0:T(8,128)}) %reduce-scatter.21.cloned.1.call-update) | async-done | bytes 73744
  1020.0 104.5 %reduce-scatter.23.cloned.1.call-done = f32[24,768]{1,0:T(8,128)} async-done(((f32[768,768]{1,0:T(8,128)}), f32[24,768]{1,0:T(8,128)}) %reduce-scatter.23.cloned.1.call-update) | async-done | bytes 73744
  1124.5 141.6 %reduce-scatter.17.cloned.1.call-done = f32[96,768]{1,0:T(8,128)} async-done(((f32[3072,768]{1,0:T(8,128)}), f32[96,768]{1,0:T(8,128)}) %reduce-scatter.17.cloned.1.call-update) | async-done | bytes 294928 | tf_op jit(solution)/shard_map/reduce_scatter | solution.py:367
  1266.1 141.6 %reduce-scatter.15.cloned.1.call-done = f32[24,3072]{1,0:T(8,128)} async-done(((f32[768,3072]{1,0:T(8,128)}), f32[24,3072]{1,0:T(8,128)}) %reduce-scatter.15.cloned.1.call-update) | async-done | bytes 294928 | tf_op jit(solution)/shard_map/reduce_scatter | solution.py:365
  (438 shorter events, 507.0 us)
Async XLA Ops:
  7.2 63.6 %all-gather.8.cloned.1.call-start = ((), (), s32[]{:S(2)}) async-start(), calls=%async_computation.8 | async-start | bytes 1216512 | tf_op jit(solution)/shard_map/all_gather | solution.py:309
  7.9 153.3 %all-gather.6.cloned.1.call-start = ((), (), s32[]{:S(2)}) async-start(), calls=%async_computation.7 | async-start | bytes 1216512 | tf_op jit(solution)/shard_map/all_gather | solution.py:308
  8.7 246.9 %all-gather.10.cloned.1.call-start = ((), (), s32[]{:S(2)}) async-start(), calls=%async_computation.9 | async-start | bytes 1216512 | tf_op jit(solution)/shard_map/all_gather | solution.py:313
  9.4 272.9 %all-gather.12.cloned.1.call-start = ((), (), s32[]{:S(2)}) async-start(), calls=%async_computation.10 | async-start | bytes 4866048 | tf_op jit(solution)/shard_map/all_gather | solution.py:317
  11.8 61.3 %all-to-all-start = ((bf16[32,24,768]{2,1,0:T(8,128)(2,1)}), bf16[32,24,768]{2,1,0:T(8,128)(2,1)S(1)}, u32[]{:S(2)}, u32[]{:S(2)}) async-start(bf16[32,24,768]{2,1,0:T(8,128)(2,1)} %stack.17), calls=%async_computation | async-start | bytes 2359296 | tf_op jit(solution)/shard_map/all_to_all | solution.py:303
  19.2 327.8 %all-gather.14.cloned.1.call-start = ((), (), s32[]{:S(2)}) async-start(), calls=%async_computation.11 | async-start | bytes 4866048 | tf_op jit(solution)/shard_map/all_gather | solution.py:319
  76.1 90.5 %collective-permute-start = (bf16[2,512,768]{2,1,0:T(8,128)(2,1)}, bf16[2,512,768]{2,1,0:T(8,128)(2,1)}, u32[]{:S(2)}, u32[]{:S(2)}) collective-permute-start(bf16[2,512,768]{2,1,0:T(8,128)(2,1)} %pad_maximum_fusion.1), channel_id=1, source_target_pairs={{0,2},{1,3},{2,4},{3,5},{4,6},{5,7},{8,10},{9,11},{10,12},{11,13},... | collective-permute-start | bytes 4718600 | tf_op jit(solution)/shard_map/ppermute | solution.py:17
  79.6 88.5 %collective-permute-start.1 = (bf16[2,512,768]{2,1,0:T(8,128)(2,1)}, bf16[2,512,768]{2,1,0:T(8,128)(2,1)}, u32[]{:S(2)}, u32[]{:S(2)}) collective-permute-start(bf16[2,512,768]{2,1,0:T(8,128)(2,1)} %pad_maximum_fusion.1), channel_id=1, source_target_pairs={{0,1},{1,2},{2,3},{3,4},{4,5},{5,6},{6,7},{8,9},{9,10},{10,11},{11... | collective-permute-start | bytes 4718600 | tf_op jit(solution)/shard_map/ppermute | solution.py:17
  84.3 85.5 %collective-permute-start.2 = (bf16[2,512,768]{2,1,0:T(8,128)(2,1)}, bf16[2,512,768]{2,1,0:T(8,128)(2,1)}, u32[]{:S(2)}, u32[]{:S(2)}) collective-permute-start(bf16[2,512,768]{2,1,0:T(8,128)(2,1)} %pad_maximum_fusion.1), channel_id=1, source_target_pairs={{1,0},{2,1},{3,2},{4,3},{5,4},{6,5},{7,6},{9,8},{10,9},{11,10},{12... | collective-permute-start | bytes 4718600 | tf_op jit(solution)/shard_map/ppermute | solution.py:17
  85.6 85.7 %collective-permute-start.3 = (bf16[2,512,768]{2,1,0:T(8,128)(2,1)}, bf16[2,512,768]{2,1,0:T(8,128)(2,1)}, u32[]{:S(2)}, u32[]{:S(2)}) collective-permute-start(bf16[2,512,768]{2,1,0:T(8,128)(2,1)} %pad_maximum_fusion.1), channel_id=1, source_target_pairs={{2,0},{3,1},{4,2},{5,3},{6,4},{7,5},{10,8},{11,9},{12,10},{13,11},... | collective-permute-start | bytes 4718600 | tf_op jit(solution)/shard_map/ppermute | solution.py:17
  86.9 905.6 %reduce-scatter.13.cloned.1.call-start = ((), (), s32[]{:S(2)}) async-start(), calls=%async_computation.12 | async-start | bytes 2433024 | tf_op jit(solution)/shard_map/reduce_scatter | solution.py:361
  373.7 37.7 %collective-permute-start.4 = (bf16[2,512,768]{2,1,0:T(8,128)(2,1)}, bf16[2,512,768]{2,1,0:T(8,128)(2,1)}, u32[]{:S(2)}, u32[]{:S(2)}) collective-permute-start(bf16[2,512,768]{2,1,0:T(8,128)(2,1)} %pad_maximum_fusion.2), channel_id=1, source_target_pairs={{0,2},{1,3},{2,4},{3,5},{4,6},{5,7},{8,10},{9,11},{10,12},{11,13},... | collective-permute-start | bytes 4718600 | tf_op jit(solution)/shard_map/ppermute | solution.py:17
  378.2 71.2 %collective-permute-start.5 = (bf16[2,512,768]{2,1,0:T(8,128)(2,1)}, bf16[2,512,768]{2,1,0:T(8,128)(2,1)}, u32[]{:S(2)}, u32[]{:S(2)}) collective-permute-start(bf16[2,512,768]{2,1,0:T(8,128)(2,1)} %pad_maximum_fusion.2), channel_id=1, source_target_pairs={{0,1},{1,2},{2,3},{3,4},{4,5},{5,6},{6,7},{8,9},{9,10},{10,11},{11... | collective-permute-start | bytes 4718600 | tf_op jit(solution)/shard_map/ppermute | solution.py:17
  382.7 68.4 %collective-permute-start.6 = (bf16[2,512,768]{2,1,0:T(8,128)(2,1)}, bf16[2,512,768]{2,1,0:T(8,128)(2,1)}, u32[]{:S(2)}, u32[]{:S(2)}) collective-permute-start(bf16[2,512,768]{2,1,0:T(8,128)(2,1)} %pad_maximum_fusion.2), channel_id=1, source_target_pairs={{1,0},{2,1},{3,2},{4,3},{5,4},{6,5},{7,6},{9,8},{10,9},{11,10},{12... | collective-permute-start | bytes 4718600 | tf_op jit(solution)/shard_map/ppermute | solution.py:17
  384.0 69.2 %collective-permute-start.7 = (bf16[2,512,768]{2,1,0:T(8,128)(2,1)}, bf16[2,512,768]{2,1,0:T(8,128)(2,1)}, u32[]{:S(2)}, u32[]{:S(2)}) collective-permute-start(bf16[2,512,768]{2,1,0:T(8,128)(2,1)} %pad_maximum_fusion.2), channel_id=1, source_target_pairs={{2,0},{3,1},{4,2},{5,3},{6,4},{7,5},{10,8},{11,9},{12,10},{13,11},... | collective-permute-start | bytes 4718600 | tf_op jit(solution)/shard_map/ppermute | solution.py:17
  645.7 346.8 %reduce-scatter.19.cloned.1.call-start = ((), (), s32[]{:S(2)}) async-start(), calls=%async_computation.15 | async-start | bytes 2433024
  807.6 212.4 %reduce-scatter.21.cloned.1.call-start = ((), (), s32[]{:S(2)}) async-start(), calls=%async_computation.16 | async-start | bytes 2433024
  820.9 40.8 %collective-permute-start.10 = (bf16[2,512,768]{1,2,0:T(8,128)(2,1)S(1)}, bf16[2,512,768]{1,2,0:T(8,128)(2,1)S(1)}, u32[]{:S(2)}, u32[]{:S(2)}) collective-permute-start(bf16[2,512,768]{1,2,0:T(8,128)(2,1)S(1)} %get-tuple-element.505), channel_id=1, source_target_pairs={{0,1},{1,2},{2,3},{3,4},{4,5},{5,6},{6,7},{8,9},{9,10},{10,11},{11... | collective-permute-start | bytes 4718600 | tf_op jit(solution)/shard_map/ppermute | solution.py:17
  824.7 37.2 %collective-permute-start.11 = (bf16[2,512,768]{1,2,0:T(8,128)(2,1)S(1)}, bf16[2,512,768]{1,2,0:T(8,128)(2,1)S(1)}, u32[]{:S(2)}, u32[]{:S(2)}) collective-permute-start(bf16[2,512,768]{1,2,0:T(8,128)(2,1)S(1)} %get-tuple-element.504), channel_id=1, source_target_pairs={{0,2},{1,3},{2,4},{3,5},{4,6},{5,7},{8,10},{9,11},{10,12},{11,13},... | collective-permute-start | bytes 4718600 | tf_op jit(solution)/shard_map/ppermute | solution.py:17
  826.3 42.8 %collective-permute-start.8 = (bf16[2,512,768]{1,2,0:T(8,128)(2,1)S(1)}, bf16[2,512,768]{1,2,0:T(8,128)(2,1)S(1)}, u32[]{:S(2)}, u32[]{:S(2)}) collective-permute-start(bf16[2,512,768]{1,2,0:T(8,128)(2,1)S(1)} %get-tuple-element.503), channel_id=1, source_target_pairs={{2,0},{3,1},{4,2},{5,3},{6,4},{7,5},{10,8},{11,9},{12,10},{13,11},... | collective-permute-start | bytes 4718600 | tf_op jit(solution)/shard_map/ppermute | solution.py:17
  827.6 41.5 %collective-permute-start.9 = (bf16[2,512,768]{1,2,0:T(8,128)(2,1)S(1)}, bf16[2,512,768]{1,2,0:T(8,128)(2,1)S(1)}, u32[]{:S(2)}, u32[]{:S(2)}) collective-permute-start(bf16[2,512,768]{1,2,0:T(8,128)(2,1)S(1)} %get-tuple-element.506), channel_id=1, source_target_pairs={{1,0},{2,1},{3,2},{4,3},{5,4},{6,5},{7,6},{9,8},{10,9},{11,10},{12... | collective-permute-start | bytes 4718600 | tf_op jit(solution)/shard_map/ppermute | solution.py:17
  877.6 246.9 %reduce-scatter.23.cloned.1.call-start = ((), (), s32[]{:S(2)}) async-start(), calls=%async_computation.17 | async-start | bytes 2433024
  884.1 382.0 %reduce-scatter.17.cloned.1.call-start = ((), (), s32[]{:S(2)}) async-start(), calls=%async_computation.14 | async-start | bytes 9732096 | tf_op jit(solution)/shard_map/reduce_scatter | solution.py:367
  892.8 515.0 %reduce-scatter.15.cloned.1.call-start = ((), (), s32[]{:S(2)}) async-start(), calls=%async_computation.13 | async-start | bytes 9732096 | tf_op jit(solution)/shard_map/reduce_scatter | solution.py:365
  (41 other events, 504.7 us)
Sparse Core Ops, SparseCore 0:
  10.9 59.8 all-gather.7
  73.8 87.4 all-gather.5
  164.2 52.7 all-gather.9
  219.8 62.4 all-gather.11
  285.1 61.8 all-gather.13
  645.8 97.1 reduce-scatter.12
  807.8 107.6 reduce-scatter.18
  921.4 98.6 reduce-scatter.20
  1025.9 98.5 reduce-scatter.22
  1130.8 135.2 reduce-scatter.16
  1272.6 135.1 reduce-scatter.14
